TPU v7x, 256 devices: a whole 4x4x8 slice. The times are simulated.
256 devices in a mesh: dp: 4 (over x), space: 16 (over z_lo, y), tm: 4 (over z_hi, core).
Axes of the slice: x: 4, y: 4, z: 8 (z_hi: 2, z_lo: 4; z = z_hi * 4 + z_lo), core: 2. Of those that a mesh axis runs over, the one named last changes fastest.
Arguments:
- inputs: bfloat16 [4, 32, 64, 4096], P('dp', 'tm', None, 'space'), may hold values from -6 to 6
- grad_out: bfloat16 [4, 32, 64, 4096], P('dp', 'tm', None, 'space'), may hold values from -6 to 6
- conv_w: bfloat16 [2, 128, 64], replicated, may hold values from -0.5 to 0.5
- conv_b: float32 [128], replicated, may hold values from -3 to 3
- mix_w: bfloat16 [3, 64, 64], replicated, may hold values from -0.4375 to 0.4375
- mix_b: float32 [64], replicated, may hold values from -3 to 3
- adj_tiles: bfloat16 [32, 8, 128, 128], P('space'), may hold values from -0.1875 to 0.1875
- tile_cols: int32 [32, 8], P('space'), may hold values from 0 to 9, as said below
- send_rows: int32 [16, 16, 64], P('space'), may hold values from 0 to 255
- counts: int32 [16, 16], P('space'), may hold values from 0 to 64, as said below
Outputs:
- outputs: bfloat16 [4, 32, 64, 4096], P('dp', 'tm', None, 'space')
- grad_inputs: bfloat16 [4, 32, 64, 4096], P('dp', 'tm', None, 'space')
- grad_conv_w: float32 [2, 128, 64], replicated
- grad_conv_b: float32 [128], replicated
- grad_mix_w: float32 [3, 64, 64], replicated
- grad_mix_b: float32 [64], replicated
Inputs may be any that keep to these rules, and one draw needn't show every extreme that they name: counts[s, s] = 0; counts[0, 1] = 64. `tile_cols`: column blocks below 2 are the part's own sensor blocks, 2 + i the i-th block of 128 received slots in order of source part and slot; in each row block the first 4 ids are below 2, the others are not.
All inputs are finite; a program needn't handle non-finite values.
Results may differ from a plain program's by a relative error of at most 0.0058.
Values may be sent and summed in bfloat16 or wider, within the bound.
A program may use at most 64 MiB of HBM per device.

v0:
```python
import math
import jax
import jax.numpy as jnp
from jax import lax
from jax.sharding import PartitionSpec as P

DILATION_SIZE = 2


def from_behind(value, axis, steps):
    count = lax.axis_size(axis)
    leading, last = (max(0, -steps), min(count, count - steps))
    return lax.ppermute(value, axis, [(source, source + steps) for source in range(leading, last)])


def slot_mask(counts, slot_count, dtype):
    slots = lax.broadcasted_iota(jnp.int32, (counts.shape[1], slot_count), 1)
    return (slots < counts[0][:, None]).astype(dtype)


def pack_rows(field, send_rows, live_slots):
    picked = field[:, :, send_rows[0]] * live_slots
    return picked.reshape(field.shape[0], field.shape[1], -1)


def tile_product(extended, adj_tiles, tile_cols):
    timestep_count, chan_count = (extended.shape[0], extended.shape[1])
    blocks = extended.reshape(timestep_count, chan_count, -1, adj_tiles.shape[2])
    picked = blocks[:, :, tile_cols]
    return jnp.einsum("tcrkj,rkij->tcri", picked, adj_tiles, preferred_element_type=jnp.float32)


def forward_start(field, send_rows, live_slots):
    packed = pack_rows(field, send_rows, live_slots)
    own_part = None
    return (packed, own_part)


def forward_finish(field, received, adj_tiles, tile_cols):
    total = tile_product(jnp.concatenate([field, received], 2), adj_tiles, tile_cols)
    return total.reshape(field.shape).astype(jnp.bfloat16)


def back_start(grad, adj_tiles, tile_cols, send_rows):
    timestep_count, chan_count, sensor_count = grad.shape
    tile_size = adj_tiles.shape[2]
    row_blocks = sensor_count // tile_size
    half_slots = tile_cols.shape[1] // 2
    halo_blocks = send_rows.shape[1] * send_rows.shape[2] // tile_size
    blocks = grad.reshape(timestep_count, chan_count, row_blocks, tile_size)
    remote_terms = jnp.einsum(
        "tcri,rkij->tcrkj", blocks, adj_tiles[:, half_slots:], preferred_element_type=jnp.float32
    )
    remote_sums = jnp.zeros((timestep_count, chan_count, halo_blocks, tile_size), jnp.float32)
    remote_sums = remote_sums.at[:, :, tile_cols[:, half_slots:] - row_blocks].add(remote_terms)
    return remote_sums.reshape(timestep_count, chan_count, -1).astype(jnp.bfloat16)


def back_finish(grad, returned, adj_tiles, tile_cols, send_rows, live_slots):
    timestep_count, chan_count, sensor_count = grad.shape
    tile_size = adj_tiles.shape[2]
    row_blocks = sensor_count // tile_size
    half_slots = tile_cols.shape[1] // 2
    blocks = grad.reshape(timestep_count, chan_count, row_blocks, tile_size)
    own_terms = jnp.einsum(
        "tcri,rkij->tcrkj", blocks, adj_tiles[:, :half_slots], preferred_element_type=jnp.float32
    )
    total = jnp.zeros((timestep_count, chan_count, row_blocks, tile_size), jnp.float32)
    total = total.at[:, :, tile_cols[:, :half_slots]].add(own_terms).reshape(grad.shape)
    returned = returned.reshape(
        timestep_count, chan_count, send_rows.shape[1], send_rows.shape[2]
    ).astype(jnp.float32)
    return total.at[:, :, send_rows[0]].add(returned * live_slots.astype(jnp.float32))


def mixing_grads(sample_grad, fields):
    grad_mix_w = jnp.stack(
        [
            jnp.einsum("ton,tcn->oc", sample_grad, item, preferred_element_type=jnp.float32)
            for item in fields
        ]
    )
    grad_mix_b = jnp.sum(sample_grad.astype(jnp.float32), axis=(0, 2))
    return (grad_mix_w, grad_mix_b)


def body(inputs, grad_out, conv_w, conv_b, mix_w, mix_b, adj_tiles, tile_cols, send_rows, counts):
    sample_input = inputs[0]
    sample_grad = grad_out[0]
    timestep_count, chan_count, sensor_count = sample_input.shape
    live_slots = slot_mask(counts, send_rows.shape[2], jnp.bfloat16)
    prior_border_slice = from_behind(sample_input[timestep_count - DILATION_SIZE :], "tm", 1)
    preceding_window = jnp.concatenate(
        [prior_border_slice, sample_input[: timestep_count - DILATION_SIZE]], 0
    )
    preact = jnp.einsum("oc,tcn->ton", conv_w[1], sample_input, preferred_element_type=jnp.float32)
    preact = preact + jnp.einsum(
        "oc,tcn->ton", conv_w[0], preceding_window, preferred_element_type=jnp.float32
    )
    preact = preact + conv_b[None, :, None]
    filtered = jnp.tanh(preact[:, :chan_count])
    gating = jax.nn.sigmoid(preact[:, chan_count:])
    hidden = (filtered * gating).astype(jnp.bfloat16)
    grad_float = sample_grad.astype(jnp.float32)
    packed_one, early_one = forward_start(hidden, send_rows, live_slots)
    received_one = lax.all_to_all(packed_one, "space", split_axis=2, concat_axis=2, tiled=True)
    hop_one = forward_finish(hidden, received_one, adj_tiles, tile_cols)
    packed_two, early_two = forward_start(hop_one, send_rows, live_slots)
    received_two = lax.all_to_all(packed_two, "space", split_axis=2, concat_axis=2, tiled=True)
    hop_two = forward_finish(hop_one, received_two, adj_tiles, tile_cols)
    fields = (hidden, hop_one, hop_two)
    grad_mix_w, grad_mix_b = mixing_grads(sample_grad, fields)
    back_two = jnp.einsum(
        "oc,ton->tcn", mix_w[2], sample_grad, preferred_element_type=jnp.float32
    ).astype(jnp.bfloat16)
    returned_two = lax.all_to_all(
        back_start(back_two, adj_tiles, tile_cols, send_rows),
        "space",
        split_axis=2,
        concat_axis=2,
        tiled=True,
    )
    back_one = jnp.einsum("oc,ton->tcn", mix_w[1], sample_grad, preferred_element_type=jnp.float32)
    back_one = (
        back_one + back_finish(back_two, returned_two, adj_tiles, tile_cols, send_rows, live_slots)
    ).astype(jnp.bfloat16)
    returned_one = lax.all_to_all(
        back_start(back_one, adj_tiles, tile_cols, send_rows),
        "space",
        split_axis=2,
        concat_axis=2,
        tiled=True,
    )
    back_hidden = jnp.einsum(
        "oc,ton->tcn", mix_w[0], sample_grad, preferred_element_type=jnp.float32
    )
    back_hidden = back_hidden + back_finish(
        back_one, returned_one, adj_tiles, tile_cols, send_rows, live_slots
    )
    mixed = sample_input.astype(jnp.float32) + mix_b[None, :, None]
    for index in range(3):
        mixed = mixed + jnp.einsum(
            "oc,tcn->ton", mix_w[index], fields[index], preferred_element_type=jnp.float32
        )
    outputs = mixed.astype(jnp.bfloat16)[None]
    grad_filter = back_hidden * (1.0 - filtered * filtered) * gating
    grad_gate = back_hidden * filtered * gating * (1.0 - gating)
    backward_preactivation = jnp.concatenate([grad_filter, grad_gate], 1).astype(jnp.bfloat16)
    next_border_slice = from_behind(backward_preactivation[:DILATION_SIZE], "tm", -1)
    following_window = jnp.concatenate(
        [backward_preactivation[DILATION_SIZE:], next_border_slice], 0
    )
    grad_inputs = grad_float + jnp.einsum(
        "oc,ton->tcn", conv_w[1], backward_preactivation, preferred_element_type=jnp.float32
    )
    grad_inputs = grad_inputs + jnp.einsum(
        "oc,ton->tcn", conv_w[0], following_window, preferred_element_type=jnp.float32
    )
    grad_inputs = grad_inputs.astype(jnp.bfloat16)[None]
    grad_conv_w = jnp.stack(
        [
            jnp.einsum(
                "ton,tcn->oc",
                backward_preactivation,
                preceding_window,
                preferred_element_type=jnp.float32,
            ),
            jnp.einsum(
                "ton,tcn->oc",
                backward_preactivation,
                sample_input,
                preferred_element_type=jnp.float32,
            ),
        ]
    )
    grad_conv_b = jnp.sum(backward_preactivation.astype(jnp.float32), axis=(0, 2))
    grad_conv_w, grad_conv_b, grad_mix_w, grad_mix_b = lax.psum(
        (grad_conv_w, grad_conv_b, grad_mix_w, grad_mix_b), ("dp", "space", "tm")
    )
    cell_count = (
        inputs.shape[0]
        * timestep_count
        * sensor_count
        * lax.axis_size("dp")
        * lax.axis_size("space")
        * lax.axis_size("tm")
    )
    scale = 1.0 / math.sqrt(cell_count)
    return (
        outputs,
        grad_inputs,
        grad_conv_w * scale,
        grad_conv_b * scale,
        grad_mix_w * scale,
        grad_mix_b * scale,
    )


def solution(mesh):
    in_specs = (
        P("dp", "tm", None, "space"),
        P("dp", "tm", None, "space"),
        P(),
        P(),
        P(),
        P(),
        P("space", None, None, None),
        P("space", None),
        P("space", None, None),
        P("space", None),
    )
    out_specs = (P("dp", "tm", None, "space"), P("dp", "tm", None, "space"), P(), P(), P(), P())
    return jax.shard_map(body, mesh=mesh, in_specs=in_specs, out_specs=out_specs, check_vma=False)
```

profile of v0, /device:TPU:1, one launch (start us, length us, event | category | flops | bytes accessed | tf_op | source)
XLA Modules:
  0.0 680.7 jit_solution(10881315894750508709)
XLA Ops:
  12.5 3.5 scatter_fusion.1
  19.6 9.2 %all-to-all-start.2 = ((bf16[16,2,16384]{2,1,0:T(2,128)(2,1)}), bf16[16,2,16384]{2,1,0:T(2,128)(2,1)}, u32[]{:S(2)}, u32[]{:S(2)}) async-start(bf16[16,2,16384]{2,1,0:T(2,128)(2,1)} %reshape.258), calls=%async_computation.2 | async-start | bytes 2097152 | tf_op jit(solution)/shard_map/all_to_all | solution.py:116
  32.5 18.7 %all-to-all-done.2 = bf16[16,2,16384]{2,1,0:T(2,128)(2,1)} async-done(((bf16[16,2,16384]{2,1,0:T(2,128)(2,1)}), bf16[16,2,16384]{2,1,0:T(2,128)(2,1)}, u32[]{:S(2)}, u32[]{:S(2)}) %all-to-all-start.2) | async-done | bytes 1048608 | tf_op jit(solution)/shard_map/all_to_all | solution.py:116
  51.2 3.8 reshape.259
  58.1 71.3 %scatter_fusion.2 = f32[8,64,256]{1,0,2:T(8,128)S(1)} fusion(f32[8,64,256]{1,0,2:T(8,128)S(1)} %copy.84, s32[1024]{0:T(1024)S(1)} %reshape.131, f32[1024,8,64]{2,1,0:T(8,128)} %bitcast.273), kind=kCustom, calls=%fused_computation.6 | custom fusion | flops 524288 | bytes 6295552 | tf_op jit(solution)/shard_map/scatter-add | solution.py:73
  132.5 3.5 scatter_fusion.4
  141.6 7.7 %all-to-all-start.3 = ((bf16[16,2,16384]{2,1,0:T(2,128)(2,1)}), bf16[16,2,16384]{2,1,0:T(2,128)(2,1)}, u32[]{:S(2)}, u32[]{:S(2)}) async-start(bf16[16,2,16384]{2,1,0:T(2,128)(2,1)} %reshape.260), calls=%async_computation.3 | async-start | bytes 2097152 | tf_op jit(solution)/shard_map/all_to_all | solution.py:127
  149.3 8.2 %collective-permute-start = (bf16[2,64,256]{2,1,0:T(8,128)(2,1)S(1)}, bf16[2,64,256]{2,1,0:T(8,128)(2,1)S(1)}, u32[]{:S(2)}, u32[]{:S(2)}) collective-permute-start(bf16[2,64,256]{2,1,0:T(8,128)(2,1)S(1)} %slice_bitcast_fusion.1), channel_id=1, source_target_pairs={{0,1},{1,2},{2,3},{4,5},{5,6},{6,7},{8,9},{9,10},{10,11},{12,13},{... | collective-permute-start | bytes 196616 | tf_op jit(solution)/shard_map/ppermute | solution.py:13
  158.2 7.7 %collective-permute-done = bf16[2,64,256]{2,1,0:T(8,128)(2,1)S(1)} collective-permute-done((bf16[2,64,256]{2,1,0:T(8,128)(2,1)S(1)}, bf16[2,64,256]{2,1,0:T(8,128)(2,1)S(1)}, u32[]{:S(2)}, u32[]{:S(2)}) %collective-permute-start) | collective-permute-done | bytes 65568 | tf_op jit(solution)/shard_map/ppermute | solution.py:13
  172.2 3.8 reshape.261
  179.0 71.3 %scatter_fusion.5 = f32[8,64,256]{1,0,2:T(8,128)S(1)} fusion(f32[8,64,256]{1,0,2:T(8,128)S(1)} %copy.92, s32[1024]{0:T(1024)S(1)} %reshape.131, f32[1024,8,64]{2,1,0:T(8,128)} %bitcast.272), kind=kCustom, calls=%fused_computation.9 | custom fusion | flops 524288 | bytes 6295552 | tf_op jit(solution)/shard_map/scatter-add | solution.py:73
  252.6 7.6 %gather_fusion = bf16[1024,8,64]{2,1,0:T(8,128)(2,1)} fusion(bf16[8,64,256]{1,0,2:T(8,128)(2,1)S(1)} %copy.63, s32[1024]{0:T(1024)S(1)} %broadcast_clamp_fusion), kind=kCustom, calls=%fused_computation | custom fusion | bytes 2101248 | tf_op jit(solution)/shard_map/gather | solution.py:22
  260.1 4.9 fusion.76
  267.3 7.9 %all-to-all-start = ((bf16[16,2,16384]{2,1,0:T(2,128)(2,1)}), bf16[16,2,16384]{2,1,0:T(2,128)(2,1)S(1)}, u32[]{:S(2)}, u32[]{:S(2)}) async-start(bf16[16,2,16384]{2,1,0:T(2,128)(2,1)} %reshape.254), calls=%async_computation | async-start | bytes 2097152 | tf_op jit(solution)/shard_map/all_to_all | solution.py:106
  276.1 21.2 %all-to-all-done = bf16[16,2,16384]{2,1,0:T(2,128)(2,1)S(1)} async-done(((bf16[16,2,16384]{2,1,0:T(2,128)(2,1)}), bf16[16,2,16384]{2,1,0:T(2,128)(2,1)S(1)}, u32[]{:S(2)}, u32[]{:S(2)}) %all-to-all-start) | async-done | bytes 1048608 | tf_op jit(solution)/shard_map/all_to_all | solution.py:106
  299.7 3.4 pad_maximum_fusion
  303.1 3.4 copy.65
  313.2 4.8 fusion.77
  318.0 4.7 reshape.256
  322.7 7.9 %all-to-all-start.1 = ((bf16[16,2,16384]{2,1,0:T(2,128)(2,1)}), bf16[16,2,16384]{2,1,0:T(2,128)(2,1)S(1)}, u32[]{:S(2)}, u32[]{:S(2)}) async-start(bf16[16,2,16384]{2,1,0:T(2,128)(2,1)} %reshape.256), calls=%async_computation.1 | async-start | bytes 2097152 | tf_op jit(solution)/shard_map/all_to_all | solution.py:109
  336.4 4.1 collective-permute-start.1
  340.7 236.7 %all-reduce.3.cloned.1.call-done = f32[2,128,64]{1,2,0:T(8,128)} async-done(((f32[2,128,64]{1,2,0:T(8,128)}), f32[2,128,64]{1,2,0:T(8,128)}) %all-reduce.3.cloned.1.call-update) | async-done | bytes 65552 | tf_op jit(solution)/shard_map/psum | solution.py:177
  585.3 3.4 pad_maximum_fusion.1
  597.1 75.0 %all-reduce = (f32[128]{0:T(128)S(1)}, f32[3,64,64]{1,2,0:T(8,128)S(1)}, f32[64]{0:T(128)S(1)}) all-reduce(f32[128]{0:T(128)S(1)} %convert_reduce_fusion, f32[3,64,64]{1,2,0:T(8,128)S(1)} %pad_maximum_fusion.6, f32[64]{0:T(128)S(1)} %convert_reduce_fusion.1), channel_id=1, replica_groups=mesh['dp'=4,'space'=16,'tm'=4] {'dp','space','tm'}, use_global_device_ids=true, to_apply=%region_8.0 | all-reduce | flops 12480 | bytes 99840 | tf_op jit(solution)/shard_map/psum | solution.py:177
  (143 shorter events, 72.3 us)
Async XLA Ops:
  17.3 11.6 %copy-start.1 = (bf16[2,8,128,128]{3,2,1,0:T(8,128)(2,1)S(1)}, bf16[2,8,128,128]{3,2,1,0:T(8,128)(2,1)}, u32[]{:S(2)}) copy-start(bf16[2,8,128,128]{3,2,1,0:T(8,128)(2,1)} %param.16) | copy-start | bytes 1572868
  19.6 31.6 %all-to-all-start.2 = ((bf16[16,2,16384]{2,1,0:T(2,128)(2,1)}), bf16[16,2,16384]{2,1,0:T(2,128)(2,1)}, u32[]{:S(2)}, u32[]{:S(2)}) async-start(bf16[16,2,16384]{2,1,0:T(2,128)(2,1)} %reshape.258), calls=%async_computation.2 | async-start | bytes 2097152 | tf_op jit(solution)/shard_map/all_to_all | solution.py:116
  139.3 10.0 %copy-start.12 = (bf16[1,8,64,256]{3,2,1,0:T(8,128)(2,1)S(1)}, bf16[1,8,64,256]{3,2,1,0:T(8,128)(2,1)}, u32[]{:S(2)}) copy-start(bf16[1,8,64,256]{3,2,1,0:T(8,128)(2,1)} %param.10) | copy-start | bytes 786436
  141.6 16.3 %copy-start.21 = (bf16[2,128,64]{1,2,0:T(8,128)(2,1)S(1)}, bf16[2,128,64]{1,2,0:T(8,128)(2,1)}, u32[]{:S(2)}) copy-start(bf16[2,128,64]{1,2,0:T(8,128)(2,1)} %param.12) | copy-start | bytes 98308
  141.6 24.3 %copy-start.26 = (f32[128]{0:T(128)S(1)}, f32[128]{0:T(128)}, u32[]{:S(2)}) copy-start(f32[128]{0:T(128)} %param.13) | copy-start | bytes 1540
  141.6 30.6 %all-to-all-start.3 = ((bf16[16,2,16384]{2,1,0:T(2,128)(2,1)}), bf16[16,2,16384]{2,1,0:T(2,128)(2,1)}, u32[]{:S(2)}, u32[]{:S(2)}) async-start(bf16[16,2,16384]{2,1,0:T(2,128)(2,1)} %reshape.260), calls=%async_computation.3 | async-start | bytes 2097152 | tf_op jit(solution)/shard_map/all_to_all | solution.py:127
  149.3 16.6 %collective-permute-start = (bf16[2,64,256]{2,1,0:T(8,128)(2,1)S(1)}, bf16[2,64,256]{2,1,0:T(8,128)(2,1)S(1)}, u32[]{:S(2)}, u32[]{:S(2)}) collective-permute-start(bf16[2,64,256]{2,1,0:T(8,128)(2,1)S(1)} %slice_bitcast_fusion.1), channel_id=1, source_target_pairs={{0,1},{1,2},{2,3},{4,5},{5,6},{6,7},{8,9},{9,10},{10,11},{12,13},{... | collective-permute-start | bytes 196616 | tf_op jit(solution)/shard_map/ppermute | solution.py:13
  157.8 8.1 %copy-start.17 = (bf16[6,64,256]{2,1,0:T(8,128)(2,1)}, bf16[6,64,256]{2,1,0:T(8,128)(2,1)S(1)}, u32[]{:S(2)}) copy-start(bf16[6,64,256]{2,1,0:T(8,128)(2,1)S(1)} %slice_bitcast_fusion) | copy-start | bytes 589828
  251.9 23.9 %copy-start.5 = (bf16[8,64,256]{2,1,0:T(8,128)(2,1)}, bf16[8,64,256]{2,1,0:T(8,128)(2,1)S(1)}, u32[]{:S(2)}) copy-start(bf16[8,64,256]{2,1,0:T(8,128)(2,1)S(1)} %get-tuple-element.27) | copy-start | bytes 786436
  251.9 23.9 %copy-start.7 = (bf16[8,64,256]{2,1,0:T(8,128)(2,1)}, bf16[8,64,256]{2,1,0:T(8,128)(2,1)S(1)}, u32[]{:S(2)}) copy-start(bf16[8,64,256]{2,1,0:T(8,128)(2,1)S(1)} %get-tuple-element.28) | copy-start | bytes 786436
  265.1 10.2 %copy-start.22 = (s32[2,8]{1,0:T(2,128)S(1)}, s32[2,8]{1,0:T(2,128)}, u32[]{:S(2)}) copy-start(s32[2,8]{1,0:T(2,128)} %param.17) | copy-start | bytes 196
  267.3 8.2 %copy-start.18 = (bf16[6,64,256]{2,1,0:T(8,128)(2,1)S(1)}, bf16[6,64,256]{2,1,0:T(8,128)(2,1)}, u32[]{:S(2)}) copy-start(bf16[6,64,256]{2,1,0:T(8,128)(2,1)} %copy-done.17) | copy-start | bytes 589828
  267.3 8.5 %copy-start.13 = (bf16[1,8,64,256]{3,2,1,0:T(8,128)(2,1)S(1)}, bf16[1,8,64,256]{3,2,1,0:T(8,128)(2,1)}, u32[]{:S(2)}) copy-start(bf16[1,8,64,256]{3,2,1,0:T(8,128)(2,1)} %param.10) | copy-start | bytes 786436
  267.3 30.0 %all-to-all-start = ((bf16[16,2,16384]{2,1,0:T(2,128)(2,1)}), bf16[16,2,16384]{2,1,0:T(2,128)(2,1)S(1)}, u32[]{:S(2)}, u32[]{:S(2)}) async-start(bf16[16,2,16384]{2,1,0:T(2,128)(2,1)} %reshape.254), calls=%async_computation | async-start | bytes 2097152 | tf_op jit(solution)/shard_map/all_to_all | solution.py:106
  318.0 13.4 %copy-start.6 = (bf16[8,64,256]{2,1,0:T(8,128)(2,1)S(1)}, bf16[8,64,256]{2,1,0:T(8,128)(2,1)}, u32[]{:S(2)}) copy-start(bf16[8,64,256]{2,1,0:T(8,128)(2,1)} %copy-done.5) | copy-start | bytes 786436
  318.0 13.4 %copy-start.8 = (bf16[8,64,256]{2,1,0:T(8,128)(2,1)S(1)}, bf16[8,64,256]{2,1,0:T(8,128)(2,1)}, u32[]{:S(2)}) copy-start(bf16[8,64,256]{2,1,0:T(8,128)(2,1)} %copy-done.7) | copy-start | bytes 786436
  322.7 8.7 %copy-start.10 = (bf16[8,64,256]{2,1,0:T(8,128)(2,1)S(1)}, bf16[8,64,256]{2,1,0:T(8,128)(2,1)}, u32[]{:S(2)}) copy-start(bf16[8,64,256]{2,1,0:T(8,128)(2,1)} %copy-done.9) | copy-start | bytes 786436
  322.7 11.3 %copy-start.14 = (bf16[1,8,64,256]{3,2,1,0:T(8,128)(2,1)S(1)}, bf16[1,8,64,256]{3,2,1,0:T(8,128)(2,1)}, u32[]{:S(2)}) copy-start(bf16[1,8,64,256]{3,2,1,0:T(8,128)(2,1)} %param.10) | copy-start | bytes 786436
  322.7 11.3 %copy-start.25 = (f32[64]{0:T(128)S(1)}, f32[64]{0:T(128)}, u32[]{:S(2)}) copy-start(f32[64]{0:T(128)} %param.15) | copy-start | bytes 772
  322.7 260.2 %all-to-all-start.1 = ((bf16[16,2,16384]{2,1,0:T(2,128)(2,1)}), bf16[16,2,16384]{2,1,0:T(2,128)(2,1)S(1)}, u32[]{:S(2)}, u32[]{:S(2)}) async-start(bf16[16,2,16384]{2,1,0:T(2,128)(2,1)} %reshape.256), calls=%async_computation.1 | async-start | bytes 2097152 | tf_op jit(solution)/shard_map/all_to_all | solution.py:109
  330.6 246.8 %all-reduce.3.cloned.1.call-start = ((), (), s32[]{:S(2)}) async-start(), calls=%async_computation.4 | async-start | bytes 131072 | tf_op jit(solution)/shard_map/psum | solution.py:177
  335.7 245.5 %copy-start.16 = (f32[8,64,256]{2,1,0:T(8,128)S(1)}, f32[8,64,256]{2,1,0:T(8,128)}, u32[]{:S(2)}) copy-start(f32[8,64,256]{2,1,0:T(8,128)} %fusion.4) | copy-start | bytes 1572868
  336.4 242.5 %collective-permute-start.1 = (bf16[2,128,256]{2,1,0:T(8,128)(2,1)}, bf16[2,128,256]{2,1,0:T(8,128)(2,1)}, u32[]{:S(2)}, u32[]{:S(2)}) collective-permute-start(bf16[2,128,256]{2,1,0:T(8,128)(2,1)} %fusion.50), channel_id=1, source_target_pairs={{1,0},{2,1},{3,2},{5,4},{6,5},{7,6},{9,8},{10,9},{11,10},{13,12},{... | collective-permute-start | bytes 393224 | tf_op jit(solution)/shard_map/ppermute | solution.py:13
  594.4 2.7 copy-start.20
  (10 other events, 14.1 us)
Sparse Core Ops, SparseCore 0:
  337.6 239.8 all-reduce.2
where the time goes:
time: 688 us; the launch traced here: 681 us
  waiting for transfers between devices  286 us (42%)
  other arithmetic  183 us (27%)
  blocking collectives  75 us (11%)
  local copies, waits for them, and re-layouts  58.8 us (9%)
  starting transfers between devices  45.2 us (7%)
  matrix products  18.1 us (3%)
  between operations  14.7 us (2%)
    psum x1, waiting for transfers between devices, body(): lax.psum((grad_conv_w, grad_conv_b, grad_mix_w, grad_mix_b), ('dp', 'spac...  237 us
    scatter-add x2, other arithmetic, back_finish(): total.at[:, :, send_rows[0]].add(returned * live_slots.astype(jnp.float32))  143 us
    psum x1, blocking collectives, body(): lax.psum((grad_conv_w, grad_conv_b, grad_mix_w, grad_mix_b), ('dp', 'spac...  75 us
    unnamed x63, local copies, waits for them, and re-layouts  26.4 us
    all_to_all x1, waiting for transfers between devices, body(): lax.all_to_all(packed_one, 'space', split_axis=2, concat_axis=2, tiled=True)  21.2 us
    all_to_all x1, waiting for transfers between devices, body(): lax.all_to_all(back_start(back_two, adj_tiles, tile_cols, send_rows), 'sp...  18.7 us
  transfers between devices with their start and end apart: 7, of which 5 were waited for; matrix products, arithmetic and copies ran while one was open for 3% of the time, Pallas kernels for 0%

commit v1 on v0

--- a/solution.py
+++ b/solution.py
@@ -5,6 +5,11 @@
 from jax.sharding import PartitionSpec as P
 
 DILATION_SIZE = 2
+
+
+def begin_tiles(payload):
+    after = lax.psum(lax.psum(payload, ("space", "tm")), "dp")
+    return after
 
 
 def from_behind(value, axis, steps):
@@ -174,8 +179,8 @@
         ]
     )
     grad_conv_b = jnp.sum(backward_preactivation.astype(jnp.float32), axis=(0, 2))
-    grad_conv_w, grad_conv_b, grad_mix_w, grad_mix_b = lax.psum(
-        (grad_conv_w, grad_conv_b, grad_mix_w, grad_mix_b), ("dp", "space", "tm")
+    grad_conv_w, grad_conv_b, grad_mix_w, grad_mix_b = begin_tiles(
+        (grad_conv_w, grad_conv_b, grad_mix_w, grad_mix_b)
     )
     cell_count = (
         inputs.shape[0]

time: 688 us -> 910 us (1.32)
  the two profiles are of different devices: /device:TPU:1 before, /device:TPU:32 now
where the time goes in v1:
time: 910 us; the launch traced here: 902 us
  blocking collectives  325 us (36%)
  waiting for transfers between devices  276 us (30%)
  other arithmetic  183 us (20%)
  local copies, waits for them, and re-layouts  58.6 us (6%)
  starting transfers between devices  27.6 us (3%)
  matrix products  17.3 us (2%)
  between operations  14.7 us (2%)
    psum x2, blocking collectives, begin_tiles(): after = lax.psum(lax.psum(payload, ('space', 'tm')), 'dp')  325 us
    psum x2, waiting for transfers between devices, begin_tiles(): after = lax.psum(lax.psum(payload, ('space', 'tm')), 'dp')  212 us
    scatter-add x2, other arithmetic, back_finish(): total.at[:, :, send_rows[0]].add(returned * live_slots.astype(jnp.float32))  143 us
    unnamed x69, local copies, waits for them, and re-layouts  26.4 us
    all_to_all x1, waiting for transfers between devices, body(): lax.all_to_all(packed_one, 'space', split_axis=2, concat_axis=2, tiled=True)  23.3 us
    all_to_all x1, waiting for transfers between devices, body(): lax.all_to_all(back_start(back_two, adj_tiles, tile_cols, send_rows), 'sp...  22.2 us
    all_to_all x1, waiting for transfers between devices, body(): lax.all_to_all(back_start(back_one, adj_tiles, tile_cols, send_rows), 'sp...  18.7 us
  transfers between devices with their start and end apart: 8, of which 5 were waited for; matrix products, arithmetic and copies ran while one was open for 2% of the time, Pallas kernels for 0%

profile of v1, /device:TPU:32, one launch (start us, length us, event | category | flops | bytes accessed | tf_op | source)
XLA Modules:
  0.0 902.5 jit_solution(10135946634033348608)
XLA Ops:
  12.5 3.5 scatter_fusion.1
  19.6 8.7 all-to-all-start.2
  31.9 22.2 %all-to-all-done.2 = bf16[16,2,16384]{2,1,0:T(2,128)(2,1)} async-done(((bf16[16,2,16384]{2,1,0:T(2,128)(2,1)}), bf16[16,2,16384]{2,1,0:T(2,128)(2,1)}, u32[]{:S(2)}, u32[]{:S(2)}) %all-to-all-start.2) | async-done | bytes 1048608 | tf_op jit(solution)/shard_map/all_to_all | solution.py:121
  54.1 3.8 reshape.259
  61.0 71.3 %scatter_fusion.2 = f32[8,64,256]{1,0,2:T(8,128)S(1)} fusion(f32[8,64,256]{1,0,2:T(8,128)S(1)} %copy.84, s32[1024]{0:T(1024)S(1)} %reshape.131, f32[1024,8,64]{2,1,0:T(8,128)} %bitcast.273), kind=kCustom, calls=%fused_computation.6 | custom fusion | flops 524288 | bytes 6295552 | tf_op jit(solution)/shard_map/scatter-add | solution.py:78
  135.4 3.5 scatter_fusion.4
  144.5 5.3 all-to-all-start.3
  156.6 18.7 %all-to-all-done.3 = bf16[16,2,16384]{2,1,0:T(2,128)(2,1)} async-done(((bf16[16,2,16384]{2,1,0:T(2,128)(2,1)}), bf16[16,2,16384]{2,1,0:T(2,128)(2,1)}, u32[]{:S(2)}, u32[]{:S(2)}) %all-to-all-start.3) | async-done | bytes 1048608 | tf_op jit(solution)/shard_map/all_to_all | solution.py:132
  175.3 3.8 reshape.261
  182.2 71.3 %scatter_fusion.5 = f32[8,64,256]{1,0,2:T(8,128)S(1)} fusion(f32[8,64,256]{1,0,2:T(8,128)S(1)} %copy.92, s32[1024]{0:T(1024)S(1)} %reshape.131, f32[1024,8,64]{2,1,0:T(8,128)} %bitcast.272), kind=kCustom, calls=%fused_computation.9 | custom fusion | flops 524288 | bytes 6295552 | tf_op jit(solution)/shard_map/scatter-add | solution.py:78
  255.7 7.6 gather_fusion
  263.3 4.9 fusion.76
  270.5 5.2 all-to-all-start
  277.2 23.3 %all-to-all-done = bf16[16,2,16384]{2,1,0:T(2,128)(2,1)S(1)} async-done(((bf16[16,2,16384]{2,1,0:T(2,128)(2,1)}), bf16[16,2,16384]{2,1,0:T(2,128)(2,1)S(1)}, u32[]{:S(2)}, u32[]{:S(2)}) %all-to-all-start) | async-done | bytes 1048608 | tf_op jit(solution)/shard_map/all_to_all | solution.py:111
  302.8 3.4 pad_maximum_fusion
  312.9 3.3 gather_fusion.2
  316.2 4.8 fusion.77
  321.0 4.7 reshape.256
  325.7 5.3 all-to-all-start.1
  334.6 167.7 %all-reduce.5.cloned.1.call-done = f32[2,128,64]{1,2,0:T(8,128)} async-done(((f32[2,128,64]{1,2,0:T(8,128)}), f32[2,128,64]{1,2,0:T(8,128)}) %all-reduce.5.cloned.1.call-update) | async-done | bytes 65552 | tf_op jit(solution)/shard_map/psum | solution.py:11
  504.8 44.3 %all-reduce.7.cloned.1.call-done = f32[2,128,64]{1,2,0:T(8,128)} async-done(((f32[2,128,64]{1,2,0:T(8,128)}), f32[2,128,64]{1,2,0:T(8,128)}) %all-reduce.7.cloned.1.call-update) | async-done | bytes 65552 | tf_op jit(solution)/shard_map/psum | solution.py:11
  557.0 3.4 pad_maximum_fusion.1
  568.7 308.0 %all-reduce = (f32[128]{0:T(128)S(1)}, f32[3,64,64]{1,2,0:T(8,128)S(1)}, f32[64]{0:T(128)S(1)}) all-reduce(f32[128]{0:T(128)S(1)} %convert_reduce_fusion, f32[3,64,64]{1,2,0:T(8,128)S(1)} %pad_maximum_fusion.6, f32[64]{0:T(128)S(1)} %convert_reduce_fusion.1), channel_id=1, replica_groups=mesh['dp'=4,'space'=16,'tm'=4] {'space','tm'}, use_global_device_ids=true, to_apply=%region_9.0 | all-reduce | flops 12480 | bytes 99840 | tf_op jit(solution)/shard_map/psum | solution.py:11
  876.7 17.1 %all-reduce.1 = (f32[128]{0:T(128)S(1)}, f32[3,64,64]{1,2,0:T(8,128)S(1)}, f32[64]{0:T(128)S(1)}) all-reduce(f32[128]{0:T(128)S(1)} %get-tuple-element.24, f32[3,64,64]{1,2,0:T(8,128)S(1)} %get-tuple-element.25, f32[64]{0:T(128)S(1)} %get-tuple-element.26), channel_id=1, replica_groups=mesh['dp'=4,'space'=16,'tm'=4] {'dp'}, use_global_device_ids=true, to_apply=%region_10.0 | all-reduce | flops 12480 | bytes 99840 | tf_op jit(solution)/shard_map/psum | solution.py:11
  (153 shorter events, 72.9 us)
Async XLA Ops:
  17.3 11.0 %copy-start.1 = (bf16[2,8,128,128]{3,2,1,0:T(8,128)(2,1)S(1)}, bf16[2,8,128,128]{3,2,1,0:T(8,128)(2,1)}, u32[]{:S(2)}) copy-start(bf16[2,8,128,128]{3,2,1,0:T(8,128)(2,1)} %param.16) | copy-start | bytes 1572868
  19.6 34.5 %all-to-all-start.2 = ((bf16[16,2,16384]{2,1,0:T(2,128)(2,1)}), bf16[16,2,16384]{2,1,0:T(2,128)(2,1)}, u32[]{:S(2)}, u32[]{:S(2)}) async-start(bf16[16,2,16384]{2,1,0:T(2,128)(2,1)} %reshape.258), calls=%async_computation.2 | async-start | bytes 2097152 | tf_op jit(solution)/shard_map/all_to_all | solution.py:121
  142.2 7.5 copy-start.12
  144.5 7.1 copy-start.21
  144.5 7.5 copy-start.29
  144.5 30.8 %all-to-all-start.3 = ((bf16[16,2,16384]{2,1,0:T(2,128)(2,1)}), bf16[16,2,16384]{2,1,0:T(2,128)(2,1)}, u32[]{:S(2)}, u32[]{:S(2)}) async-start(bf16[16,2,16384]{2,1,0:T(2,128)(2,1)} %reshape.260), calls=%async_computation.3 | async-start | bytes 2097152 | tf_op jit(solution)/shard_map/all_to_all | solution.py:132
  149.8 2.2 collective-permute-start
  255.0 21.2 %copy-start.5 = (bf16[8,64,256]{2,1,0:T(8,128)(2,1)}, bf16[8,64,256]{2,1,0:T(8,128)(2,1)S(1)}, u32[]{:S(2)}) copy-start(bf16[8,64,256]{2,1,0:T(8,128)(2,1)S(1)} %get-tuple-element.30) | copy-start | bytes 786436
  255.0 21.2 %copy-start.7 = (bf16[8,64,256]{2,1,0:T(8,128)(2,1)}, bf16[8,64,256]{2,1,0:T(8,128)(2,1)S(1)}, u32[]{:S(2)}) copy-start(bf16[8,64,256]{2,1,0:T(8,128)(2,1)S(1)} %get-tuple-element.31) | copy-start | bytes 786436
  268.2 7.5 copy-start.25
  270.5 5.5 copy-start.23
  270.5 5.8 copy-start.13
  270.5 30.0 %all-to-all-start = ((bf16[16,2,16384]{2,1,0:T(2,128)(2,1)}), bf16[16,2,16384]{2,1,0:T(2,128)(2,1)S(1)}, u32[]{:S(2)}, u32[]{:S(2)}) async-start(bf16[16,2,16384]{2,1,0:T(2,128)(2,1)} %reshape.254), calls=%async_computation | async-start | bytes 2097152 | tf_op jit(solution)/shard_map/all_to_all | solution.py:111
  321.0 10.0 %copy-start.24 = (f32[1,128,64]{1,2,0:T(8,128)S(1)}, f32[1,128,64]{1,2,0:T(8,128)}, u32[]{:S(2)}) copy-start(f32[1,128,64]{1,2,0:T(8,128)} %convolution_bitcast_fusion.13) | copy-start | bytes 98308
  321.0 10.7 %copy-start.10 = (bf16[8,64,256]{2,1,0:T(8,128)(2,1)S(1)}, bf16[8,64,256]{2,1,0:T(8,128)(2,1)}, u32[]{:S(2)}) copy-start(bf16[8,64,256]{2,1,0:T(8,128)(2,1)} %copy-done.9) | copy-start | bytes 786436
  325.7 6.9 copy-start.6
  325.7 6.9 copy-start.8
  325.7 7.9 copy-start.14
  325.7 7.9 copy-start.28
  325.7 228.9 %all-to-all-start.1 = ((bf16[16,2,16384]{2,1,0:T(2,128)(2,1)}), bf16[16,2,16384]{2,1,0:T(2,128)(2,1)S(1)}, u32[]{:S(2)}, u32[]{:S(2)}) async-start(bf16[16,2,16384]{2,1,0:T(2,128)(2,1)} %reshape.256), calls=%async_computation.1 | async-start | bytes 2097152 | tf_op jit(solution)/shard_map/all_to_all | solution.py:114
  331.0 171.4 %all-reduce.5.cloned.1.call-start = ((), (), s32[]{:S(2)}) async-start(), calls=%async_computation.4 | async-start | bytes 131072 | tf_op jit(solution)/shard_map/psum | solution.py:11
  331.7 217.4 %all-reduce.7.cloned.1.call-start = ((), (), s32[]{:S(2)}) async-start(), calls=%async_computation.5 | async-start | bytes 131072 | tf_op jit(solution)/shard_map/psum | solution.py:11
  334.6 218.3 %copy-start.16 = (f32[8,64,256]{2,1,0:T(8,128)S(1)}, f32[8,64,256]{2,1,0:T(8,128)}, u32[]{:S(2)}) copy-start(f32[8,64,256]{2,1,0:T(8,128)} %fusion.4) | copy-start | bytes 1572868
  503.0 47.6 %collective-permute-start.1 = (bf16[2,128,256]{2,1,0:T(8,128)(2,1)}, bf16[2,128,256]{2,1,0:T(8,128)(2,1)}, u32[]{:S(2)}, u32[]{:S(2)}) collective-permute-start(bf16[2,128,256]{2,1,0:T(8,128)(2,1)} %fusion.50), channel_id=1, source_target_pairs={{1,0},{2,1},{3,2},{5,4},{6,5},{7,6},{9,8},{10,9},{11,10},{13,12},{... | collective-permute-start | bytes 393224 | tf_op jit(solution)/shard_map/ppermute | solution.py:18
  (14 other events, 25.3 us)
Sparse Core Ops, SparseCore 0:
  335.8 166.4 all-reduce.4
  504.6 44.4 all-reduce.6
